TPU v7x, 32 devices: a whole 2x2x4 slice. The times are simulated.
32 devices in a mesh: cfg: 2 (over y), ta: 8 (over z, x), sa: 2 (over core).
Axes of the slice: x: 2, y: 2, z: 4, core: 2. Of those that a mesh axis runs over, the one named last changes fastest.
Arguments:
- forward: bfloat16 [32, 2, 256, 2, 256], P(('cfg', 'ta'), 'sa'), parts along dimension 0, may hold values from -6 to 6
- backward: bfloat16 [4, 16, 256, 2, 256], P(('cfg', 'sa'), 'ta'), parts along dimension 0, may hold values from -6 to 6
- sink_bank: bfloat16 [32, 9, 256, 2, 256], P(('cfg', 'ta'), None, 'sa'), parts along dimension 0, may hold values from -0.25 to 0.25
- source_bank: bfloat16 [4, 9, 256, 2, 256], P(('cfg', 'sa'), None, 'ta'), parts along dimension 0, may hold values from -0.25 to 0.25
- op_mom: int32 [4], replicated, may hold values from 0 to 2
- op_disp: int32 [4], replicated, may hold values from 0 to 2
Outputs:
- correlator: float32 [32, 2, 2, 4, 4], P(('cfg', 'ta'), 'sa'), parts along dimension 0
There are 2 independent parts, one for each index of `cfg`. A program takes and returns all parts, laid end to end along the dimension named above; an argument that names none is the same for every part. Nothing has to cross between parts.
All inputs are finite; a program needn't handle non-finite values.
Results may differ from a plain program's by a relative error of at most 0.0029.
Values may be sent and summed in bfloat16 or wider, within the bound.
A program may use at most 64 MiB of HBM per device.

v0:
```python
import jax
import jax.numpy as jnp
from jax import lax
from jax.sharding import PartitionSpec as P

NDISP = 3
NBANK = 9


def select_ops(bank, op_mom, op_disp):
    wanted = op_mom * NDISP + op_disp
    onehot = (wanted[:, None] == jnp.arange(NBANK, dtype=jnp.int32)[None, :]).astype(jnp.bfloat16)
    chosen = jnp.einsum("ak,tkrcp->tarcp", onehot, bank, preferred_element_type=jnp.float32)
    return chosen.astype(jnp.bfloat16)


def sink_factor(forward_local):
    real_part = forward_local[:, :, 0, :]
    imag_part = forward_local[:, :, 1, :]
    upper = jnp.concatenate([real_part, imag_part], axis=2)
    lower = jnp.concatenate([-imag_part, real_part], axis=2)
    return jnp.concatenate([upper, lower], axis=1)


def sink_product(factor, chosen):
    merged = chosen.reshape(chosen.shape[0], chosen.shape[1], chosen.shape[2], -1)
    result = jnp.einsum("tarv,tvw->tarw", merged, factor, preferred_element_type=jnp.float32)
    return result.astype(jnp.bfloat16)


def source_columns(stacked_back, chosen):
    real_part = chosen[:, :, 0, :]
    imag_part = chosen[:, :, 1, :]
    for_real = jnp.concatenate([real_part, -imag_part], axis=2)
    for_imag = jnp.concatenate([imag_part, real_part], axis=2)
    joined = jnp.stack([for_real, for_imag], axis=0)
    return jnp.einsum("tui,xaju->taxij", stacked_back, joined, preferred_element_type=jnp.float32)


def per_device(forward, backward, sink_bank, source_bank, op_mom, op_disp):
    factor = sink_factor(forward[:, 0])
    back_local = backward[0]
    stacked_back = jnp.concatenate([back_local[:, :, 0, :], back_local[:, :, 1, :]], axis=1)
    sink_local = select_ops(sink_bank, op_mom, op_disp)
    source_local = select_ops(source_bank, op_mom, op_disp)
    product = sink_product(factor, lax.all_gather(sink_local, "sa", axis=2, tiled=True))
    reverse = source_columns(
        stacked_back, lax.all_gather(source_local, "ta", axis=2, tiled=True)[0]
    )
    order = product.shape[2]
    reshaped = product.reshape(product.shape[0], product.shape[1], order, 2, order)
    paired = jnp.einsum(
        "taicj,tbdij->tabcd",
        reshaped,
        reverse,
        preferred_element_type=jnp.float32,
        precision=lax.Precision.HIGHEST,
    )
    real_trace = paired[..., 0, 0] - paired[..., 1, 1]
    imag_trace = paired[..., 0, 1] + paired[..., 1, 0]
    correlator = jnp.stack([real_trace, imag_trace], axis=1) / order
    return correlator[:, None]


def solution(mesh):
    placed = (
        P(("cfg", "ta"), "sa", None, None, None),
        P(("cfg", "sa"), "ta", None, None, None),
        P(("cfg", "ta"), None, "sa", None, None),
        P(("cfg", "sa"), None, "ta", None, None),
        P(),
        P(),
    )
    return jax.shard_map(
        per_device,
        mesh=mesh,
        in_specs=placed,
        out_specs=P(("cfg", "ta"), "sa", None, None, None),
        check_vma=False,
    )
```

profile of v0, /device:TPU:0, one launch (start us, length us, event | category | flops | bytes accessed | tf_op | source)
XLA Modules:
  0.0 118.9 jit_solution(14901242579871128287)
XLA Ops:
  6.5 0.8 multiply_add_fusion
  7.4 1.9 %fusion.12 = bf16[1,4,32,2,256]{4,1,3,0,2:T(4,128)(2,1)} fusion(bf16[9,32,2,256]{3,2,1,0:T(2,128)(2,1)} %bitcast.90, s32[4]{0:T(128)S(1)} %multiply_add_fusion), kind=kOutput, calls=%fused_computation.12 | convolution fusion | flops 1245220 | bytes 426000 | tf_op jit(solution)/shard_map/ak,tkrcp->tarcp/dot_general | solution.py:13
  9.3 0.0 all-gather.5.cloned.1.call-start
  9.4 2.6 %fusion.9 = bf16[2,4,128,2,256]{4,1,3,2,0:T(4,128)(2,1)} fusion(bf16[2,9,128,2,256]{4,3,2,1,0:T(2,128)(2,1)S(1)} %copy-done, s32[4]{0:T(128)S(1)} %multiply_add_fusion), kind=kOutput, calls=%fused_computation.10 | convolution fusion | flops 9961508 | bytes 3407888 | tf_op jit(solution)/shard_map/ak,tkrcp->tarcp/dot_general | solution.py:13
  12.0 0.0 all-gather.5.cloned.1.call-update
  12.0 0.1 copy.66
  12.1 0.9 copy-done.2
  13.0 0.1 copy.65
  13.1 0.8 slice_bitcast_fusion.5
  13.9 38.6 %all-gather.3.cloned.1.call-done = bf16[1,4,256,2,256]{4,1,3,0,2:T(4,128)(2,1)} async-done(((bf16[1,4,32,2,256]{4,1,3,0,2:T(4,128)(2,1)}), bf16[1,4,256,2,256]{4,1,3,0,2:T(4,128)(2,1)}) %all-gather.3.cloned.1.call-update) | async-done | bytes 1048592 | tf_op jit(solution)/shard_map/all_gather | solution.py:48
  52.5 1.4 %copy.64 = bf16[1,4,256,2,256]{4,2,1,3,0:T(8,128)(2,1)S(1)} copy(bf16[1,4,256,2,256]{4,1,3,0,2:T(4,128)(2,1)} %all-gather.3.cloned.1.call-done) | data formatting | bytes 2097152 | tf_op jit(solution)/shard_map/all_gather | solution.py:48
  54.0 0.1 slice_bitcast_fusion
  54.1 0.2 maximum_bitcast_fusion.2
  54.2 0.8 copy-done.3
  55.0 3.2 %convolution_bitcast_fusion = f32[2,4,2,256,256,1]{3,4,0,1,2,5:T(8,128)} fusion(bf16[1,4,256,512]{3,2,1,0:T(8,128)(2,1)S(1)} %get-tuple-element.12, bf16[1,4,256,512]{3,2,1,0:T(8,128)(2,1)S(1)} %get-tuple-element.11, bf16[2,256,256]{2,1,0:T(8,128)(2,1)S(1)} %copy-done.3, bf16[2,256,256]{2,1,0:T(8,128)(2,1)S(1)} %get-tuple-element.9), kind=kOutput, calls=%fused_computation.2 | convolution fusion | flops 1078984704 | bytes 6815744 | tf_op jit(solution)/shard_map/tui,xaju->taxij/dot_general | solution.py:37
  58.2 5.6 %copy.46 = f32[2,4,2,256,256,1]{4,1,3,5,2,0:T(4,128)} copy(f32[2,4,2,256,256,1]{3,4,0,1,2,5:T(8,128)} %convolution_bitcast_fusion) | data formatting | bytes 8388608 | tf_op jit(solution)/shard_map/tui,xaju->taxij/transpose | solution.py:37
  63.9 4.3 %copy.32 = bf16[2,4,256,2,256]{2,4,3,1,0:T(8,128)(2,1)} copy(bf16[2,4,256,2,256]{4,1,3,2,0:T(4,128)(2,1)} %all-gather.5.cloned.1.call-done) | data formatting | bytes 4194304 | tf_op jit(solution)/shard_map/all_gather | solution.py:46
  68.2 4.2 %convolution_convert_fusion = bf16[2,4,256,512]{3,2,1,0:T(8,128)(2,1)} fusion(bf16[2,4,256,512]{2,3,1,0:T(8,128)(2,1)} %bitcast.88, bf16[2,256,256]{2,1,0:T(8,128)(2,1)S(1)} %get-tuple-element.8, bf16[2,256,256]{2,1,0:T(8,128)(2,1)S(1)} %fusion.30, bf16[2,256,256]{2,1,0:T(8,128)(2,1)S(1)} %get-tuple-element.7), kind=kOutput, calls=%fused_computation.8 | convolution fusion | flops 1078984704 | bytes 4980736 | tf_op jit(solution)/shard_map/tarv,tvw->tarw/dot_general | solution.py:27
  72.4 4.0 %reshape.93 = bf16[2,4,256,2,256]{4,3,2,1,0:T(2,128)(2,1)} reshape(bf16[2,4,256,512]{3,2,1,0:T(8,128)(2,1)} %convolution_convert_fusion) | data formatting | bytes 4194304 | tf_op jit(solution)/shard_map/reshape | solution.py:51
  76.4 34.7 %fusion.4 = f32[2,4,2,4,2,1]{1,4,5,3,2,0:T(2,128)S(1)} fusion(f32[2,4,2,256,256,1]{4,1,3,5,2,0:T(4,128)} %copy.46, bf16[2,4,256,2,256]{4,3,2,1,0:T(2,128)(2,1)} %reshape.93), kind=kOutput, calls=%fused_computation.6 | convolution fusion | flops 100663296 | bytes 6291968 | tf_op jit(solution)/shard_map/taicj,tbdij->tabcd/dot_general | solution.py:52
  111.1 0.1 copy.48
  111.3 0.1 copy.38
  111.4 0.1 copy.37
  111.5 0.6 copy.39
  (14 shorter events, 0.1 us)
Async XLA Ops:
  6.5 2.8 %copy-start = (bf16[2,9,128,2,256]{4,3,2,1,0:T(2,128)(2,1)S(1)}, bf16[2,9,128,2,256]{4,3,2,1,0:T(2,128)(2,1)}, u32[]{:S(2)}) copy-start(bf16[2,9,128,2,256]{4,3,2,1,0:T(2,128)(2,1)} %param.8) | copy-start | bytes 7077892
  6.5 46.0 %all-gather.3.cloned.1.call-start = ((), (), s32[]{:S(2)}) async-start(), calls=%async_computation | async-start | bytes 1179648 | tf_op jit(solution)/shard_map/all_gather | solution.py:48
  9.3 2.7 %copy-start.1 = (bf16[1,2,256,2,256]{4,3,2,1,0:T(2,128)(2,1)S(1)}, bf16[1,2,256,2,256]{4,3,2,1,0:T(2,128)(2,1)}, u32[]{:S(2)}) copy-start(bf16[1,2,256,2,256]{4,3,2,1,0:T(2,128)(2,1)} %param.7) | copy-start | bytes 1572868
  9.3 54.5 %all-gather.5.cloned.1.call-start = ((), (), s32[]{:S(2)}) async-start(), calls=%async_computation.1 | async-start | bytes 3145728 | tf_op jit(solution)/shard_map/all_gather | solution.py:46
  12.0 1.0 copy-start.2
  54.0 1.0 copy-start.3
Sparse Core Ops, SparseCore 0:
  9.5 42.9 all-gather.2
  54.0 9.2 all-gather.4
where the time goes:
time: 119 us
  matrix products  46.7 us (39%)
  waiting for transfers between devices  38.6 us (32%)
  local copies, waits for them, and re-layouts  19 us (16%)
  between operations  13.5 us (11%)
    all_gather x1, waiting for transfers between devices, per_device(): lax.all_gather(source_local, 'ta', axis=2, tiled=True)[0]  38.6 us
    dot_general x1, matrix products, per_device(): jnp.einsum('taicj,tbdij->tabcd', reshaped, reverse, preferred_element_typ...  34.7 us
    transpose x1, local copies, waits for them, and re-layouts, source_columns(): jnp.einsum('tui,xaju->taxij', stacked_back, joined, preferred_element_typ...  5.64 us
    dot_general x2, matrix products, select_ops(): jnp.einsum('ak,tkrcp->tarcp', onehot, bank, preferred_element_type=jnp.fl...  4.49 us
    all_gather x1, local copies, waits for them, and re-layouts, per_device(): lax.all_gather(sink_local, 'sa', axis=2, tiled=True)  4.32 us
    dot_general x1, matrix products, sink_product(): jnp.einsum('tarv,tvw->tarw', merged, factor, preferred_element_type=jnp.f...  4.23 us
    reshape x1, local copies, waits for them, and re-layouts, per_device(): product.reshape(product.shape[0], product.shape[1], order, 2, order)  3.98 us
    dot_general x1, matrix products, source_columns(): jnp.einsum('tui,xaju->taxij', stacked_back, joined, preferred_element_typ...  3.22 us
  transfers between devices with their start and end apart: 2, of which 1 were waited for; matrix products, arithmetic and copies ran while one was open for 12% of the time, Pallas kernels for 0%

commit v1 on v0

v1 whole, which is shorter than its diff:
```python
import functools

import jax
import jax.numpy as jnp
from jax import lax
from jax.experimental import pallas as pl
from jax.experimental.pallas import tpu as pltpu
from jax.sharding import PartitionSpec as P

NDISP = 3
STRIP = 16
LANES = 128
F32 = jnp.float32
BF16 = jnp.bfloat16
MESH = pl.DeviceIdType.MESH


def split_parts(block):
    return pltpu.einshape("rpc->prc", block)


def dot_nt(left, right):
    return lax.dot_general(left, right, (((1,), (1,)), ((), ())), preferred_element_type=F32)


def kernel(gather, groups, mom, disp, fwd_hbm, back_hbm, sink_hbm, source_hbm, out, fwd, back, bank, src_bank,
           ops, left_mat, right_mat, prod, turned, source, acc, in_sem, s_send, s_recv, z_send, z_recv, x_send, x_recv):
    times, nop = ops.shape[0], ops.shape[1]
    half = bank.shape[2]
    size = fwd.shape[1]
    blocks, rows = source.shape[0], source.shape[3]
    sa = lax.axis_index("sa")
    me = lax.axis_index("ta")
    group, side = me // 2, lax.rem(me, 2)
    peers = [lax.rem(group + d, groups) * 2 + side for d in range(1, groups)] if gather else []
    origins = [lax.rem(group - d + groups, groups) * 2 + side for d in range(1, groups)] if gather else []
    cross = group * 2 + 1 - side

    loads = []
    for k, (a, b) in enumerate([(source_hbm, src_bank), (sink_hbm, bank), (fwd_hbm, fwd), (back_hbm, back)]):
        loads.append(pltpu.make_async_copy(a, b, in_sem.at[k]))
        loads[-1].start()

    barrier = pltpu.get_barrier_semaphore()
    pl.semaphore_signal(barrier, inc=1, device_id={"sa": 1 - sa}, device_id_type=MESH)
    if gather:
        for peer in peers + [cross]:
            pl.semaphore_signal(barrier, inc=1, device_id={"ta": peer}, device_id_type=MESH)

    index = [mom[a] * NDISP + disp[a] for a in range(nop)]
    loads[0].wait()
    if gather:
        for b in range(nop):
            source[me, b] = split_parts(src_bank[0, index[b]])
    pl.semaphore_wait(barrier, 1 + len(peers) + (1 if gather else 0))

    sends = []

    def send_source(block, b, target, send_sem, recv_sem):
        copy = pltpu.make_async_remote_copy(
            src_ref=source.at[block, b], dst_ref=source.at[block, b], send_sem=send_sem, recv_sem=recv_sem,
            device_id={"ta": target}, device_id_type=MESH)
        copy.start()
        sends.append(copy)

    if gather:
        for b in range(nop):
            send_source(me, b, cross, x_send.at[0, b], x_recv.at[0, b])
            for d in range(1, groups):
                send_source(me, b, peers[d - 1], z_send.at[d - 1, b], z_recv.at[d - 1, b])

    mine = pl.ds(pl.multiple_of(sa * half, half), half)
    loads[1].wait()
    swaps = []
    for t in range(times):
        for a in range(nop):
            parts = split_parts(bank[t, index[a]])
            for p in range(2):
                ops[t, a, mine, p * size:(p + 1) * size] = parts[p]
    for t in range(times):
        swaps.append(pltpu.make_async_remote_copy(
            src_ref=ops.at[t, :, mine], dst_ref=ops.at[t, :, mine], send_sem=s_send.at[t], recv_sem=s_recv.at[t],
            device_id={"sa": 1 - sa}, device_id_type=MESH))
        swaps[-1].start()

    loads[2].wait()
    for t in range(times):
        parts = split_parts(fwd[t])
        real, imag = parts[0].T, parts[1].T
        left_mat[t, :size, :size] = real
        left_mat[t, :size, size:] = -imag
        left_mat[t, size:, :size] = imag
        left_mat[t, size:, size:] = real
    loads[3].wait()
    for t in range(times):
        parts = split_parts(back[t])
        right_mat[t, :size, :size] = parts[0]
        right_mat[t, :size, size:] = -parts[1]
        right_mat[t, size:, :size] = parts[1]
        right_mat[t, size:, size:] = parts[0]

    acc[...] = jnp.zeros_like(acc)

    def arrived(recv_sem, block, b):
        pltpu.make_async_copy(source.at[block, b], source.at[block, b], recv_sem).wait()

    relays = [(d, b) for b in range(nop) for d in range(1, groups)] if gather else []

    def relay(count):
        for _ in range(min(count, len(relays))):
            d, b = relays.pop(0)
            arrived(z_recv.at[d - 1, b], origins[d - 1], b)
            send_source(origins[d - 1], b, cross, x_send.at[d, b], x_recv.at[d, b])

    for t in range(times):
        swaps[t].wait()
        for a in range(nop):
            result = dot_nt(left_mat[t], ops[t, a]).astype(BF16)
            prod[a, :, :size] = result[:size]
            prod[a, :, size:] = result[size:]
            if t > 0:
                relay(1)
        for a in range(nop):
            turned[t, a] = dot_nt(prod[a], right_mat[t])
            relay(1)

    def contract(block):
        for t in range(times):
            def strip(k, carry):
                carry = list(carry)
                row = pl.multiple_of(k * STRIP, STRIP)
                here = pl.ds(pl.multiple_of(block * rows + k * STRIP, STRIP), STRIP)
                for lane in range(0, size, LANES):
                    ts = [[source[block, b, p, pl.ds(row, STRIP), lane:lane + LANES].astype(F32) for p in range(2)]
                          for b in range(nop)]
                    for a in range(nop):
                        wr = turned[t, a, here, lane:lane + LANES]
                        wi = turned[t, a, here, size + lane:size + lane + LANES]
                        for b in range(nop):
                            tr, ti = ts[b]
                            re = wr * tr - wi * ti
                            im = wr * ti + wi * tr
                            at = a * nop + b
                            carry[at] = carry[at] + (re[:8] + re[8:])
                            carry[nop * nop + at] = carry[nop * nop + at] + (im[:8] + im[8:])
                return tuple(carry)

            start = tuple(acc[t, j] for j in range(2 * nop * nop))
            done = lax.fori_loop(0, rows // STRIP, strip, start)
            for j in range(2 * nop * nop):
                acc[t, j] = done[j]

    if gather:
        contract(me)
        relay(len(relays))
        for d in range(1, groups):
            contract(origins[d - 1])
        for d in range(groups):
            block = cross if d == 0 else lax.rem(group - d + groups, groups) * 2 + 1 - side
            for b in range(nop):
                arrived(x_recv.at[d, b], block, b)
            contract(block)
        for copy in sends:
            copy.wait_send()
    else:
        for k in range(blocks):
            source[k] = src_bank[k]
        lax.fori_loop(0, blocks, lambda k, c: (contract(k), c)[1], 0)

    for t in range(times):
        total = jnp.sum(jnp.sum(acc[t], axis=1), axis=1, keepdims=True) / size
        out[t] = jnp.broadcast_to(total, out.shape[1:])


def per_device(peers, forward, backward, sink_bank, source_bank, op_mom, op_disp):
    times, size = forward.shape[0], forward.shape[2]
    half, nop = sink_bank.shape[2], op_mom.shape[0]
    rows = source_bank.shape[2]
    gather = rows % STRIP == 0 and peers % 2 == 0 and peers > 2
    groups = peers // 2 if gather else 2
    blocks = peers
    if not gather:
        chosen = jnp.take(source_bank[0], op_mom * NDISP + op_disp, axis=0)
        chosen = lax.all_gather(chosen, "ta", axis=1, tiled=True)
        blocks, rows = size // STRIP, STRIP
        source_bank = chosen.reshape(nop, blocks, rows, 2, size).transpose(1, 0, 3, 2, 4)
    smem = pl.BlockSpec(memory_space=pltpu.SMEM)
    hbm = pl.BlockSpec(memory_space=pl.ANY)
    dma = pltpu.SemaphoreType.DMA
    result = pl.pallas_call(
        functools.partial(kernel, gather, groups),
        out_shape=jax.ShapeDtypeStruct((times, 2 * nop * nop, LANES), F32),
        in_specs=[smem, smem, hbm, hbm, hbm, hbm],
        out_specs=pl.BlockSpec(memory_space=pltpu.VMEM),
        scratch_shapes=[
            pltpu.VMEM((times, size, 2, size), BF16),
            pltpu.VMEM((times, size, 2, size), BF16),
            pltpu.VMEM(sink_bank.shape, BF16),
            pltpu.VMEM(source_bank.shape, BF16),
            pltpu.VMEM((times, nop, size, 2 * size), BF16),
            pltpu.VMEM((times, 2 * size, 2 * size), BF16),
            pltpu.VMEM((times, 2 * size, 2 * size), BF16),
            pltpu.VMEM((nop, size, 2 * size), BF16),
            pltpu.VMEM((times, nop, size, 2 * size), F32),
            pltpu.VMEM((blocks, nop, 2, rows, size), BF16),
            pltpu.VMEM((times, 2 * nop * nop, 8, LANES), F32),
            dma((4,)),
            dma((times,)),
            dma((times,)),
            dma((groups - 1, nop)),
            dma((groups - 1, nop)),
            dma((groups, nop)),
            dma((groups, nop)),
        ],
        compiler_params=pltpu.CompilerParams(collective_id=0, has_side_effects=True, vmem_limit_bytes=48 << 20),
    )(op_mom, op_disp, forward[:, 0], backward[0], sink_bank, source_bank)
    return result[:, :, 0].reshape(times, 1, 2, nop, nop)


def solution(mesh):
    placed = (
        P(("cfg", "ta"), "sa", None, None, None),
        P(("cfg", "sa"), "ta", None, None, None),
        P(("cfg", "ta"), None, "sa", None, None),
        P(("cfg", "sa"), None, "ta", None, None),
        P(),
        P(),
    )
    return jax.shard_map(
        functools.partial(per_device, mesh.shape["ta"]),
        mesh=mesh,
        in_specs=placed,
        out_specs=P(("cfg", "ta"), "sa", None, None, None),
        check_vma=False,
    )
```

time: 119 us -> 30.3 us (0.25)
  matrix products: 46.7 us -> 0 us
  waiting for transfers between devices: 38.6 us -> 0 us
  Pallas kernels: 0 us -> 23.2 us
  between operations: 13.5 us -> 0.02 us
  local copies, waits for them, and re-layouts: 19 us -> 6.8 us
    dot_general x5 -> x0, matrix products: 46.7 us -> none  [the longest x1 34.7 us: per_device(): jnp.einsum('taicj,tbdij->tabcd', reshaped, reverse, preferred_element_typ...]
    all_gather x2 -> x0, waiting for transfers between devices: 38.6 us -> none  [the longest x1 38.6 us: per_device(): lax.all_gather(source_local, 'ta', axis=2, tiled=True)[0]]
    pallas_call x0 -> x1, Pallas kernels: none -> 23.2 us  [per_device(): pl.pallas_call(functools.partial(kernel, gather, groups), out_shape=jax.S...]
    all_gather x2 -> x0, local copies, waits for them, and re-layouts: 5.75 us -> none  [the longest x1 4.32 us: per_device(): lax.all_gather(sink_local, 'sa', axis=2, tiled=True)]
    transpose x1 -> x0, local copies, waits for them, and re-layouts: 5.64 us -> none  [source_columns(): jnp.einsum('tui,xaju->taxij', stacked_back, joined, preferred_element_typ...]
    unnamed x10 -> x12, local copies, waits for them, and re-layouts: 1.84 us -> 6.02 us
    reshape x1 -> x0, local copies, waits for them, and re-layouts: 3.98 us -> none  [per_device(): product.reshape(product.shape[0], product.shape[1], order, 2, order)]
  transfers between devices with their start and end apart: 2 -> 0, of which waited for: 1 -> 0; matrix products, arithmetic and copies ran while one was open for 12% -> 0% of each run, Pallas kernels for 0% -> 0%
where the time goes in v1:
time: 30.3 us; the launch traced here: 30 us
  Pallas kernels  23.2 us (77%)
  local copies, waits for them, and re-layouts  6.8 us (22%)
    pallas_call x1, Pallas kernels, per_device(): pl.pallas_call(functools.partial(kernel, gather, groups), out_shape=jax.S...  23.2 us
    unnamed x12, local copies, waits for them, and re-layouts  6.02 us
    another operation x1, local copies, waits for them, and re-layouts, per_device(): return result[:, :, 0].reshape(times, 1, 2, nop, nop)  0.7 us

profile of v1, /device:TPU:0, one launch (start us, length us, event | category | flops | bytes accessed | tf_op | source)
XLA Modules:
  0.0 30.0 jit_solution(13049258149356733408)
XLA Ops:
  0.0 0.0 copy-start
  0.0 1.7 %copy-done = bf16[2,9,128,2,256]{4,3,2,1,0:T(2,128)(2,1)S(1)} copy-done((bf16[2,9,128,2,256]{4,3,2,1,0:T(2,128)(2,1)S(1)}, bf16[2,9,128,2,256]{4,3,2,1,0:T(2,128)(2,1)}, u32[]{:S(2)}) %copy-start) | copy-done | bytes 2359320
  1.7 0.0 copy-start.1
  1.7 1.0 %copy-done.1 = bf16[2,1,256,2,256]{4,3,2,1,0:T(2,128)(2,1)S(1)} copy-done((bf16[2,1,256,2,256]{4,3,2,1,0:T(2,128)(2,1)S(1)}, bf16[2,1,256,2,256]{4,3,2,1,0:T(2,128)(2,1)}, u32[]{:S(2)}) %copy-start.1) | copy-done | bytes 524312
  2.7 0.0 copy-start.2
  2.7 1.0 %copy-done.2 = bf16[1,2,256,2,256]{4,3,2,1,0:T(2,128)(2,1)S(1)} copy-done((bf16[1,2,256,2,256]{4,3,2,1,0:T(2,128)(2,1)S(1)}, bf16[1,2,256,2,256]{4,3,2,1,0:T(2,128)(2,1)}, u32[]{:S(2)}) %copy-start.2) | copy-done | bytes 524312
  3.8 0.0 copy-start.3
  3.8 1.0 %copy-done.3 = bf16[1,9,32,2,256]{4,3,2,1,0:T(2,128)(2,1)S(1)} copy-done((bf16[1,9,32,2,256]{4,3,2,1,0:T(2,128)(2,1)S(1)}, bf16[1,9,32,2,256]{4,3,2,1,0:T(2,128)(2,1)}, u32[]{:S(2)}) %copy-start.3) | copy-done | bytes 294936
  4.7 0.0 copy-start.4
  4.7 0.7 %copy-done.4 = s32[4]{0:T(128)S(1)} copy-done((s32[4]{0:T(128)S(1)}, s32[4]{0:T(128)}, u32[]{:S(2)}) %copy-start.4) | copy-done | bytes 40
  5.4 0.0 copy-start.5
  5.4 0.7 %copy-done.5 = s32[4]{0:T(128)S(1)} copy-done((s32[4]{0:T(128)S(1)}, s32[4]{0:T(128)}, u32[]{:S(2)}) %copy-start.5) | copy-done | bytes 40
  6.0 23.2 %shard_map.64 = f32[2,32,128]{2,1,0:T(8,128)S(1)} custom-call(s32[4]{0:T(128)S(1)} %copy-done.4, s32[4]{0:T(128)S(1)} %copy-done.5, bf16[2,256,2,256]{3,2,1,0:T(2,128)(2,1)S(1)} %bitcast.3, bf16[2,256,2,256]{3,2,1,0:T(2,128)(2,1)S(1)} %bitcast.4, bf16[2,9,128,2,256]{4,3,2,1,0:T(2,128)(2,1)S(1)} %copy-done, bf16[1,9,32,2,256]{4,3,2,1,0:T(2,128)(2,1)S(1)} %copy-done.3), custom_call_target="tpu_custom_call" | custom-call | tf_op jit(solution)/shard_map/pallas_call | solution.py:190
  29.2 0.1 slice_reduce_fusion
  29.3 0.7 %reshape_squeeze.3 = f32[2,1,2,4,4]{4,3,2,0,1:T(4,128)} reshape(f32[2,32]{1,0:T(2,128)S(1)} %slice_reduce_fusion) | data formatting | bytes 512 | tf_op jit(solution)/shard_map/reshape;squeeze | solution.py:217
Async XLA Ops:
  0.0 1.7 %copy-start = (bf16[2,9,128,2,256]{4,3,2,1,0:T(2,128)(2,1)S(1)}, bf16[2,9,128,2,256]{4,3,2,1,0:T(2,128)(2,1)}, u32[]{:S(2)}) copy-start(bf16[2,9,128,2,256]{4,3,2,1,0:T(2,128)(2,1)} %sink_hbm.1) | copy-start | bytes 7077892
  1.7 1.0 %copy-start.1 = (bf16[2,1,256,2,256]{4,3,2,1,0:T(2,128)(2,1)S(1)}, bf16[2,1,256,2,256]{4,3,2,1,0:T(2,128)(2,1)}, u32[]{:S(2)}) copy-start(bf16[2,1,256,2,256]{4,3,2,1,0:T(2,128)(2,1)} %param.6) | copy-start | bytes 1572868
  2.7 1.0 %copy-start.2 = (bf16[1,2,256,2,256]{4,3,2,1,0:T(2,128)(2,1)S(1)}, bf16[1,2,256,2,256]{4,3,2,1,0:T(2,128)(2,1)}, u32[]{:S(2)}) copy-start(bf16[1,2,256,2,256]{4,3,2,1,0:T(2,128)(2,1)} %param.7) | copy-start | bytes 1572868
  3.8 1.0 %copy-start.3 = (bf16[1,9,32,2,256]{4,3,2,1,0:T(2,128)(2,1)S(1)}, bf16[1,9,32,2,256]{4,3,2,1,0:T(2,128)(2,1)}, u32[]{:S(2)}) copy-start(bf16[1,9,32,2,256]{4,3,2,1,0:T(2,128)(2,1)} %source_hbm.1) | copy-start | bytes 884740
  4.7 0.7 %copy-start.4 = (s32[4]{0:T(128)S(1)}, s32[4]{0:T(128)}, u32[]{:S(2)}) copy-start(s32[4]{0:T(128)} %mom.1) | copy-start | bytes 52
  5.4 0.7 %copy-start.5 = (s32[4]{0:T(128)S(1)}, s32[4]{0:T(128)}, u32[]{:S(2)}) copy-start(s32[4]{0:T(128)} %disp.1) | copy-start | bytes 52

commit v2 on v1

--- a/solution.py
+++ b/solution.py
@@ -140,9 +140,9 @@
                             tr, ti = ts[b]
                             re = wr * tr - wi * ti
                             im = wr * ti + wi * tr
-                            at = a * nop + b
+                            at = 2 * nop * b + a
                             carry[at] = carry[at] + (re[:8] + re[8:])
-                            carry[nop * nop + at] = carry[nop * nop + at] + (im[:8] + im[8:])
+                            carry[nop + at] = carry[nop + at] + (im[:8] + im[8:])
                 return tuple(carry)
 
             start = tuple(acc[t, j] for j in range(2 * nop * nop))
@@ -169,7 +169,12 @@
 
     for t in range(times):
         total = jnp.sum(jnp.sum(acc[t], axis=1), axis=1, keepdims=True) / size
-        out[t] = jnp.broadcast_to(total, out.shape[1:])
+        lane = lax.broadcasted_iota(jnp.int32, (2 * nop, LANES), 1)
+        placed = jnp.zeros((2 * nop, LANES), F32)
+        for b in range(nop):
+            placed = jnp.where(lane == b, total[2 * nop * b:2 * nop * (b + 1)], placed)
+        for c in range(2):
+            out[t, c] = placed[nop * c:nop * (c + 1)]
 
 
 def per_device(peers, forward, backward, sink_bank, source_bank, op_mom, op_disp):
@@ -185,11 +190,11 @@
         blocks, rows = size // STRIP, STRIP
         source_bank = chosen.reshape(nop, blocks, rows, 2, size).transpose(1, 0, 3, 2, 4)
     smem = pl.BlockSpec(memory_space=pltpu.SMEM)
-    hbm = pl.BlockSpec(memory_space=pl.ANY)
+    hbm = pl.BlockSpec(memory_space=pltpu.HBM)
     dma = pltpu.SemaphoreType.DMA
     result = pl.pallas_call(
         functools.partial(kernel, gather, groups),
-        out_shape=jax.ShapeDtypeStruct((times, 2 * nop * nop, LANES), F32),
+        out_shape=jax.ShapeDtypeStruct((times, 2, nop, LANES), F32),
         in_specs=[smem, smem, hbm, hbm, hbm, hbm],
         out_specs=pl.BlockSpec(memory_space=pltpu.VMEM),
         scratch_shapes=[
@@ -212,9 +217,9 @@
             dma((groups, nop)),
             dma((groups, nop)),
         ],
-        compiler_params=pltpu.CompilerParams(collective_id=0, has_side_effects=True, vmem_limit_bytes=48 << 20),
+        compiler_params=pltpu.CompilerParams(collective_id=0, has_side_effects=True),
     )(op_mom, op_disp, forward[:, 0], backward[0], sink_bank, source_bank)
-    return result[:, :, 0].reshape(times, 1, 2, nop, nop)
+    return result[:, None, :, :, :nop]
 
 
 def solution(mesh):

time: 30.3 us -> 24.7 us (0.82)
  local copies, waits for them, and re-layouts: 6.8 us -> 1.3 us
    unnamed x12 -> x0, local copies, waits for them, and re-layouts: 6.02 us -> none
    broadcast_in_dim x0 -> x1, local copies, waits for them, and re-layouts: none -> 1.3 us  [per_device(): return result[:, None, :, :, :nop]]
    another operation x1 -> x0, local copies, waits for them, and re-layouts: 0.7 us -> none  [per_device(): return result[:, :, 0].reshape(times, 1, 2, nop, nop)]
where the time goes in v2:
time: 24.7 us; the launch traced here: 24.5 us
  Pallas kernels  23.2 us (94%)
  local copies, waits for them, and re-layouts  1.3 us (5%)
    pallas_call x1, Pallas kernels, per_device(): pl.pallas_call(functools.partial(kernel, gather, groups), out_shape=jax.S...  23.2 us
    broadcast_in_dim x1, local copies, waits for them, and re-layouts, per_device(): return result[:, None, :, :, :nop]  1.3 us

profile of v2, /device:TPU:0, one launch (start us, length us, event | category | flops | bytes accessed | tf_op | source)
XLA Modules:
  0.0 24.5 jit_solution(875065042886956750)
XLA Ops:
  0.0 23.2 %shard_map.64 = f32[2,2,4,128]{3,2,1,0:T(4,128)} custom-call(s32[4]{0:T(128)} %mom.1, s32[4]{0:T(128)} %disp.1, bf16[2,256,2,256]{3,2,1,0:T(2,128)(2,1)} %bitcast.6, bf16[2,256,2,256]{3,2,1,0:T(2,128)(2,1)} %bitcast.7, bf16[2,9,128,2,256]{4,3,2,1,0:T(2,128)(2,1)} %sink_hbm.1, bf16[1,9,32,2,256]{4,3,2,1,0:T(2,128)(2,1)} %source_hbm.1), custom_call_target="tpu_custom_call" | custom-call | tf_op jit(solution)/shard_map/pallas_call | solution.py:195
  23.2 1.3 %slice_bitcast_fusion = f32[2,1,2,4,4]{4,3,2,1,0:T(4,128)} fusion(f32[2,2,4,128]{3,2,1,0:T(4,128)} %shard_map.64), kind=kLoop, calls=%fused_computation | loop fusion | bytes 512 | tf_op jit(solution)/shard_map/broadcast_in_dim | solution.py:222

commit v3 on v2

--- a/solution.py
+++ b/solution.py
@@ -32,8 +32,14 @@
     sa = lax.axis_index("sa")
     me = lax.axis_index("ta")
     group, side = me // 2, lax.rem(me, 2)
-    peers = [lax.rem(group + d, groups) * 2 + side for d in range(1, groups)] if gather else []
-    origins = [lax.rem(group - d + groups, groups) * 2 + side for d in range(1, groups)] if gather else []
+    steps = (1, -1)
+
+    def inside(g):
+        return jnp.logical_and(g >= 0, g < groups)
+
+    def device(g, s):
+        return g * 2 + s
+
     cross = group * 2 + 1 - side
 
     loads = []
@@ -44,30 +50,41 @@
     barrier = pltpu.get_barrier_semaphore()
     pl.semaphore_signal(barrier, inc=1, device_id={"sa": 1 - sa}, device_id_type=MESH)
     if gather:
-        for peer in peers + [cross]:
-            pl.semaphore_signal(barrier, inc=1, device_id={"ta": peer}, device_id_type=MESH)
+        pl.semaphore_signal(barrier, inc=1, device_id={"ta": cross}, device_id_type=MESH)
+        for step in steps:
+            @pl.when(inside(group + step))
+            def _(step=step):
+                pl.semaphore_signal(barrier, inc=1, device_id={"ta": device(group + step, side)}, device_id_type=MESH)
 
     index = [mom[a] * NDISP + disp[a] for a in range(nop)]
     loads[0].wait()
     if gather:
         for b in range(nop):
             source[me, b] = split_parts(src_bank[0, index[b]])
-    pl.semaphore_wait(barrier, 1 + len(peers) + (1 if gather else 0))
+    greeted = 1
+    if gather:
+        greeted = 2 + sum(inside(group + step).astype(jnp.int32) for step in steps)
+    pl.semaphore_wait(barrier, greeted)
 
     sends = []
 
-    def send_source(block, b, target, send_sem, recv_sem):
+    def send_source(block, b, target, send_sem, recv_sem, when):
         copy = pltpu.make_async_remote_copy(
             src_ref=source.at[block, b], dst_ref=source.at[block, b], send_sem=send_sem, recv_sem=recv_sem,
             device_id={"ta": target}, device_id_type=MESH)
         copy.start()
-        sends.append(copy)
-
-    if gather:
-        for b in range(nop):
-            send_source(me, b, cross, x_send.at[0, b], x_recv.at[0, b])
-            for d in range(1, groups):
-                send_source(me, b, peers[d - 1], z_send.at[d - 1, b], z_recv.at[d - 1, b])
+        sends.append((when, copy))
+
+    def forward_source(block, b, j, step, hop, when):
+        @pl.when(when)
+        def _():
+            send_source(block, b, device(group + step, side), z_send.at[j, hop, b], z_recv.at[j, hop, b], when)
+
+    if gather:
+        for b in range(nop):
+            send_source(me, b, cross, x_send.at[0, b], x_recv.at[0, b], None)
+            for j, step in enumerate(steps):
+                forward_source(me, b, j, step, 0, inside(group + step))
 
     mine = pl.ds(pl.multiple_of(sa * half, half), half)
     loads[1].wait()
@@ -104,13 +121,24 @@
     def arrived(recv_sem, block, b):
         pltpu.make_async_copy(source.at[block, b], source.at[block, b], recv_sem).wait()
 
-    relays = [(d, b) for b in range(nop) for d in range(1, groups)] if gather else []
+    relays = [(hop, b, j) for hop in range(groups - 1) for b in range(nop) for j in range(2)] if gather else []
+
+    def origin(j, hop):
+        return group - steps[j] * (hop + 1)
 
     def relay(count):
         for _ in range(min(count, len(relays))):
-            d, b = relays.pop(0)
-            arrived(z_recv.at[d - 1, b], origins[d - 1], b)
-            send_source(origins[d - 1], b, cross, x_send.at[d, b], x_recv.at[d, b])
+            hop, b, j = relays.pop(0)
+            came = inside(origin(j, hop))
+            block = device(origin(j, hop), side)
+
+            @pl.when(came)
+            def _():
+                arrived(z_recv.at[j, hop, b], block, b)
+                at = 1 + 2 * hop + j
+                send_source(block, b, cross, x_send.at[at, b], x_recv.at[at, b], came)
+                if hop + 1 < groups - 1:
+                    forward_source(block, b, j, steps[j], hop + 1, inside(group + steps[j]))
 
     for t in range(times):
         swaps[t].wait()
@@ -118,8 +146,7 @@
             result = dot_nt(left_mat[t], ops[t, a]).astype(BF16)
             prod[a, :, :size] = result[:size]
             prod[a, :, size:] = result[size:]
-            if t > 0:
-                relay(1)
+            relay(1)
         for a in range(nop):
             turned[t, a] = dot_nt(prod[a], right_mat[t])
             relay(1)
@@ -152,16 +179,43 @@
 
     if gather:
         contract(me)
-        relay(len(relays))
-        for d in range(1, groups):
-            contract(origins[d - 1])
-        for d in range(groups):
-            block = cross if d == 0 else lax.rem(group - d + groups, groups) * 2 + 1 - side
-            for b in range(nop):
-                arrived(x_recv.at[d, b], block, b)
-            contract(block)
-        for copy in sends:
-            copy.wait_send()
+        for hop in range(groups - 1):
+            while relays and relays[0][0] <= hop:
+                relay(1)
+            for j in range(2):
+                relay(2)
+                @pl.when(inside(origin(j, hop)))
+                def _():
+                    contract(device(origin(j, hop), side))
+        for hop in range(-1, groups - 1):
+            for j in range(2 if hop >= 0 else 1):
+                def receive(at, block):
+                    for b in range(nop):
+                        arrived(x_recv.at[at, b], block, b)
+                    contract(block)
+
+                if hop < 0:
+                    receive(0, cross)
+                else:
+                    @pl.when(inside(origin(j, hop)))
+                    def _():
+                        receive(1 + 2 * hop + j, device(origin(j, hop), 1 - side))
+        for when, copy in sends:
+            if when is None:
+                copy.wait_send()
+        for b in range(nop):
+            for j, step in enumerate(steps):
+                for hop in range(-1, groups - 1):
+                    came = inside(origin(j, hop))
+                    if hop >= 0:
+                        @pl.when(came)
+                        def _():
+                            at = 1 + 2 * hop + j
+                            pltpu.make_async_copy(source.at[me, b], source.at[me, b], x_send.at[at, b]).wait()
+                    if hop + 1 < groups - 1:
+                        @pl.when(jnp.logical_and(came, inside(group + step)))
+                        def _():
+                            pltpu.make_async_copy(source.at[me, b], source.at[me, b], z_send.at[j, hop + 1, b]).wait()
     else:
         for k in range(blocks):
             source[k] = src_bank[k]
@@ -212,10 +266,10 @@
             dma((4,)),
             dma((times,)),
             dma((times,)),
-            dma((groups - 1, nop)),
-            dma((groups - 1, nop)),
-            dma((groups, nop)),
-            dma((groups, nop)),
+            dma((2, groups - 1, nop)),
+            dma((2, groups - 1, nop)),
+            dma((2 * groups - 1, nop)),
+            dma((2 * groups - 1, nop)),
         ],
         compiler_params=pltpu.CompilerParams(collective_id=0, has_side_effects=True),
     )(op_mom, op_disp, forward[:, 0], backward[0], sink_bank, source_bank)

time: 24.7 us -> 23.5 us (0.951)
  Pallas kernels: 23.2 us -> 22 us
    pallas_call x1, Pallas kernels: 23.2 us -> 22 us  [per_device(): pl.pallas_call(functools.partial(kernel, gather, groups), out_shape=jax.S...]
where the time goes in v3:
time: 23.5 us; the launch traced here: 23.3 us
  Pallas kernels  22 us (94%)
  local copies, waits for them, and re-layouts  1.3 us (6%)
    pallas_call x1, Pallas kernels, per_device(): pl.pallas_call(functools.partial(kernel, gather, groups), out_shape=jax.S...  22 us
    broadcast_in_dim x1, local copies, waits for them, and re-layouts, per_device(): return result[:, None, :, :, :nop]  1.3 us

profile of v3, /device:TPU:0, one launch (start us, length us, event | category | flops | bytes accessed | tf_op | source)
XLA Modules:
  0.0 23.3 jit_solution(18359303785114268417)
XLA Ops:
  0.0 22.0 %shard_map.64 = f32[2,2,4,128]{3,2,1,0:T(4,128)} custom-call(s32[4]{0:T(128)} %mom.1, s32[4]{0:T(128)} %disp.1, bf16[2,256,2,256]{3,2,1,0:T(2,128)(2,1)} %bitcast.6, bf16[2,256,2,256]{3,2,1,0:T(2,128)(2,1)} %bitcast.7, bf16[2,9,128,2,256]{4,3,2,1,0:T(2,128)(2,1)} %sink_hbm.1, bf16[1,9,32,2,256]{4,3,2,1,0:T(2,128)(2,1)} %source_hbm.1), custom_call_target="tpu_custom_call" | custom-call | tf_op jit(solution)/shard_map/pallas_call | solution.py:249
  22.0 1.3 %slice_bitcast_fusion = f32[2,1,2,4,4]{4,3,2,1,0:T(4,128)} fusion(f32[2,2,4,128]{3,2,1,0:T(4,128)} %shard_map.64), kind=kLoop, calls=%fused_computation | loop fusion | bytes 512 | tf_op jit(solution)/shard_map/broadcast_in_dim | solution.py:276

commit v4 on v3

--- a/solution.py
+++ b/solution.py
@@ -146,7 +146,8 @@
             result = dot_nt(left_mat[t], ops[t, a]).astype(BF16)
             prod[a, :, :size] = result[:size]
             prod[a, :, size:] = result[size:]
-            relay(1)
+            if t > 0:
+                relay(1)
         for a in range(nop):
             turned[t, a] = dot_nt(prod[a], right_mat[t])
             relay(1)

time: 23.5 us -> 23.7 us (level)
  no operation moved by 1% of the time
where the time goes in v4:
time: 23.7 us; the launch traced here: 23.5 us
  Pallas kernels  22.2 us (94%)
  local copies, waits for them, and re-layouts  1.3 us (5%)
    pallas_call x1, Pallas kernels, per_device(): pl.pallas_call(functools.partial(kernel, gather, groups), out_shape=jax.S...  22.2 us
    broadcast_in_dim x1, local copies, waits for them, and re-layouts, per_device(): return result[:, None, :, :, :nop]  1.3 us

profile of v4, /device:TPU:0, one launch (start us, length us, event | category | flops | bytes accessed | tf_op | source)
XLA Modules:
  0.0 23.5 jit_solution(1844753748468306878)
XLA Ops:
  0.0 22.2 %shard_map.64 = f32[2,2,4,128]{3,2,1,0:T(4,128)} custom-call(s32[4]{0:T(128)} %mom.1, s32[4]{0:T(128)} %disp.1, bf16[2,256,2,256]{3,2,1,0:T(2,128)(2,1)} %bitcast.6, bf16[2,256,2,256]{3,2,1,0:T(2,128)(2,1)} %bitcast.7, bf16[2,9,128,2,256]{4,3,2,1,0:T(2,128)(2,1)} %sink_hbm.1, bf16[1,9,32,2,256]{4,3,2,1,0:T(2,128)(2,1)} %source_hbm.1), custom_call_target="tpu_custom_call" | custom-call | tf_op jit(solution)/shard_map/pallas_call | solution.py:250
  22.2 1.3 %slice_bitcast_fusion = f32[2,1,2,4,4]{4,3,2,1,0:T(4,128)} fusion(f32[2,2,4,128]{3,2,1,0:T(4,128)} %shard_map.64), kind=kLoop, calls=%fused_computation | loop fusion | bytes 512 | tf_op jit(solution)/shard_map/broadcast_in_dim | solution.py:277
